TPU v7x, 512 devices: a whole 4x4x16 slice. The times are simulated.
512 devices in a mesh: seq: 32 (over z, core), head: 16 (over x, y).
Axes of the slice: x: 4, y: 4, z: 16, core: 2. Of those that a mesh axis runs over, the one named last changes fastest.
Arguments:
- tokens: bfloat16 [8192, 4096], P('seq', 'head'), may hold values from -40 to 40
- norm_gain: float32 [4096], replicated, may hold values from 1.5 to 8
- w_qkv: bfloat16 [4096, 3, 2048], P(None, None, 'head'), may hold values from -0.09375 to 0.09375
- w_out: bfloat16 [2048, 4096], P('head'), may hold values from -0.75 to 0.75
- span_order: int32 [64], replicated, may hold values from 0 to 63, each once
- frame_id: int32 [8192], replicated, may hold values from 0 to 63, never falling along the last dimension, each value on 1 to 256 neighbouring positions
- camera_id: int32 [8192], replicated, may hold values from 0 to 5
Outputs:
- mixed: bfloat16 [8192, 4096], P('seq', 'head')
Inputs may be any that keep to these rules, and one draw needn't show every extreme that they name: `span_order`: each of the 64 spans appears once. `frame_id`: never falls along the sequence; every frame has 1 to 256 positions and one has exactly 256.
All inputs are finite; a program needn't handle non-finite values.
Results may differ from a plain program's by a relative error of at most 0.015.
The roundings to bfloat16 on the way count: a program that leaves them out, or rounds other values in their place, can miss the bound.
Values may be sent and summed in bfloat16 or wider, within the bound.
No kernel may reach another device: no remote copies, remote signals or barrier semaphores. Data moves between devices by JAX's collectives and lax.ppermute only.
A program may use at most 64 MiB of HBM per device.

v0:
```python
import jax
import jax.numpy as jnp
from jax import lax
from jax.sharding import PartitionSpec as P

D = 4096
HD = 128


epsilon = 1e-06
key_block = 1024


def stored_order(id_table, span_order):
    span_count = span_order.shape[0]
    return id_table.reshape(span_count, -1)[span_order].reshape(-1)


def visible_pairs(query_frames, query_cameras, key_frames, key_cameras):
    earlier = key_frames[None, :] < query_frames[:, None]
    same_view = (key_frames[None, :] == query_frames[:, None]) & (
        key_cameras[None, :] == query_cameras[:, None]
    )
    return earlier | same_view


def on_device(tokens, norm_gain, w_qkv, w_out, span_order, frame_id, camera_id):
    gathered = lax.all_gather(tokens, "head", axis=1, tiled=True)
    widened = gathered.astype(jnp.float32)
    inverse = lax.rsqrt(jnp.mean(widened * widened, axis=1, keepdims=True) + epsilon)
    normed = (widened * inverse * norm_gain).astype(jnp.bfloat16)
    row_count = tokens.shape[0]
    local_heads = w_out.shape[0] // HD
    projected = jnp.dot(
        normed, w_qkv.reshape(D, 3 * local_heads * HD), preferred_element_type=jnp.float32
    )
    projected = projected.astype(jnp.bfloat16).reshape(row_count, 3, local_heads, HD)
    queries = projected[:, 0]
    key_rows = projected[:, 1].reshape(row_count, local_heads * HD)
    value_rows = projected[:, 2].reshape(row_count, local_heads * HD)
    frames = stored_order(frame_id, span_order)
    cameras = stored_order(camera_id, span_order)
    first_row = lax.axis_index("seq") * row_count
    query_frames = lax.dynamic_slice_in_dim(frames, first_row, row_count, 0)
    query_cameras = lax.dynamic_slice_in_dim(cameras, first_row, row_count, 0)
    score_scale = HD ** (-0.5)

    def absorb(running, block_keys, block_values, key_start, frame_table, camera_table):
        key_count = block_keys.shape[0]
        key_frames = lax.dynamic_slice_in_dim(frame_table, key_start, key_count, 0)
        key_cameras = lax.dynamic_slice_in_dim(camera_table, key_start, key_count, 0)
        old_best, running_total, weighted = running
        scores = (
            jnp.einsum(
                "qhd,khd->hqk",
                queries,
                block_keys.reshape(key_count, local_heads, HD),
                preferred_element_type=jnp.float32,
            )
            * score_scale
        )
        allowed = visible_pairs(query_frames, query_cameras, key_frames, key_cameras)[None]
        block_best = jnp.max(jnp.where(allowed, scores, -jnp.inf), axis=2)
        new_best = jnp.maximum(old_best, block_best)
        weights = jnp.exp(jnp.where(allowed, scores - new_best[:, :, None], -jnp.inf))
        factor = jnp.exp(old_best - new_best)
        running_total = running_total * factor + jnp.sum(weights, axis=2)
        added = jnp.einsum(
            "hqk,khd->hqd",
            weights.astype(jnp.bfloat16),
            block_values.reshape(key_count, local_heads, HD),
            preferred_element_type=jnp.float32,
        )
        weighted = weighted * factor[:, :, None] + added
        return (new_best, running_total, weighted)

    initial = (
        jnp.full((local_heads, row_count), -1e30, jnp.float32),
        jnp.zeros((local_heads, row_count), jnp.float32),
        jnp.zeros((local_heads, row_count, HD), jnp.float32),
    )
    all_keys, all_values = (
        lax.all_gather(key_rows, "seq", axis=0, tiled=True),
        lax.all_gather(value_rows, "seq", axis=0, tiled=True),
    )
    running = initial
    length = all_keys.shape[0]
    block_rows = min(key_block, length)
    full_blocks = length // block_rows

    def advance(block_index, current):
        offset = block_index * block_rows
        block_keys = lax.dynamic_slice_in_dim(all_keys, offset, block_rows, 0)
        block_values = lax.dynamic_slice_in_dim(all_values, offset, block_rows, 0)
        return absorb(current, block_keys, block_values, 0 + offset, frames, cameras)

    running = lax.fori_loop(0, full_blocks, advance, running)
    attended = (running[2] / running[1][:, :, None]).astype(jnp.bfloat16)
    partial_value = jnp.einsum(
        "hqd,hde->qe",
        attended,
        w_out.reshape(local_heads, HD, D),
        preferred_element_type=jnp.float32,
    )
    mixed_rows = lax.psum_scatter(
        partial_value.astype(jnp.bfloat16), "head", scatter_dimension=1, tiled=True
    )
    return mixed_rows


def solution(mesh):
    placed = (P("seq", "head"), P(), P(None, None, "head"), P("head", None), P(), P(), P())
    return jax.shard_map(
        on_device, mesh=mesh, in_specs=placed, out_specs=P("seq", "head"), check_vma=False
    )
```

profile of v0, /device:TPU:6, one launch (start us, length us, event | category | flops | bytes accessed | tf_op | source)
XLA Modules:
  0.0 355.3 jit_solution(11500444099656653798)
XLA Ops:
  7.3 4.7 %copy.11 = bf16[4096,3,128]{0,2,1:T(8,128)(2,1)} copy(bf16[4096,3,128]{2,0,1:T(8,128)(2,1)} %param.11) | data formatting | bytes 6291456 | tf_op args[2]
  12.0 64.8 %all-gather.6.cloned.1.call-done = bf16[256,4096]{1,0:T(8,128)(2,1)} async-done(((bf16[256,256]{1,0:T(8,128)(2,1)}), bf16[256,4096]{1,0:T(8,128)(2,1)}) %all-gather.6.cloned.1.call-update) | async-done | bytes 2097168 | tf_op jit(solution)/shard_map/all_gather | solution.py:28
  76.8 2.2 fusion.16
  79.1 3.3 fusion.23
  85.5 70.4 %all-gather.10.cloned.1.call-done = bf16[8192,1,1,128]{0,3,1,2:T(8,128)(2,1)} async-done(((bf16[256,1,1,128]{0,3,1,2:T(8,128)(2,1)}), bf16[8192,1,1,128]{0,3,1,2:T(8,128)(2,1)}) %all-gather.10.cloned.1.call-update) | async-done | bytes 2097168 | tf_op jit(solution)/shard_map/all_gather | solution.py:84
  156.0 70.8 %all-gather.8.cloned.1.call-done = bf16[8192,1,1,128]{0,3,1,2:T(8,128)(2,1)} async-done(((bf16[256,1,1,128]{0,3,1,2:T(8,128)(2,1)}), bf16[8192,1,1,128]{0,3,1,2:T(8,128)(2,1)}) %all-gather.8.cloned.1.call-update) | async-done | bytes 2097168 | tf_op jit(solution)/shard_map/all_gather | solution.py:83
  226.8 33.6 %while.18 = (s32[]{:T(128)}, f32[1,256]{1,0:T(1,128)S(1)}, f32[1,256]{1,0:T(1,128)S(1)}, f32[1,256,128]{2,1,0:T(8,128)S(1)}, s32[8192]{0:T(1024)S(1)}, /*index=5...) while((s32[]{:T(128)}, f32[1,256]{1,0:T(1,128)S(1)}, ...), condition=%wide.region_4.5_spmd.clone, body=%wide.region_1.4_spmd.clone.sunk | while | flops 140608768 | bytes 4061407 | solution.py:97
  226.8 1.7 select_reduce_fusion.2
  229.3 1.7 fusion.41
  231.0 1.8 select_reduce_fusion.2
  233.5 1.7 fusion.41
  235.2 1.8 select_reduce_fusion.2
  237.7 1.7 fusion.41
  239.4 1.8 select_reduce_fusion.2
  241.9 1.7 fusion.41
  243.6 1.8 select_reduce_fusion.2
  246.1 1.7 fusion.41
  247.8 1.8 select_reduce_fusion.2
  250.3 1.7 fusion.41
  252.1 1.8 select_reduce_fusion.2
  256.3 1.8 select_reduce_fusion.2
  258.8 1.7 fusion.41
  260.5 2.1 convolution_convert_fusion
  262.6 86.2 %reduce-scatter.2.cloned.1.call-done = bf16[256,256]{1,0:T(8,128)(2,1)} async-done(((bf16[256,4096]{1,0:T(8,128)(2,1)}), bf16[256,256]{1,0:T(8,128)(2,1)}) %reduce-scatter.2.cloned.1.call-update) | async-done | bytes 131088 | tf_op jit(solution)/shard_map/reduce_scatter | solution.py:105
  (82 shorter events, 11.3 us)
Async XLA Ops:
  6.5 253.9 %copy-start = (bf16[128,4096]{1,0:T(8,128)(2,1)S(1)}, bf16[128,4096]{1,0:T(8,128)(2,1)}, u32[]{:S(2)}) copy-start(bf16[128,4096]{1,0:T(8,128)(2,1)} %param.12) | copy-start | bytes 3145732
  6.5 70.2 %all-gather.6.cloned.1.call-start = ((), (), s32[]{:S(2)}) async-start(), calls=%async_computation.1 | async-start | bytes 2228224 | tf_op jit(solution)/shard_map/all_gather | solution.py:28
  7.3 148.7 %all-gather.10.cloned.1.call-start = ((), (), s32[]{:S(2)}) async-start(), calls=%async_computation.4 | async-start | bytes 2162688 | tf_op jit(solution)/shard_map/all_gather | solution.py:84
  7.3 71.7 %copy-start.4 = (f32[4096]{0:T(1024)S(1)}, f32[4096]{0:T(1024)}, u32[]{:S(2)}) copy-start(f32[4096]{0:T(1024)} %param.10) | copy-start | bytes 49156
  76.8 2.3 copy-start.3
  79.0 5.0 %copy-start.5 = (s32[64]{0:T(128)S(1)}, s32[64]{0:T(128)}, u32[]{:S(2)}) copy-start(s32[64]{0:T(128)} %param.13) | copy-start | bytes 772
  79.0 5.0 %copy-start.1 = (s32[8192]{0:T(1024)S(1)}, s32[8192]{0:T(1024)}, u32[]{:S(2)}) copy-start(s32[8192]{0:T(1024)} %param.15) | copy-start | bytes 98308
  79.0 5.6 %copy-start.2 = (s32[8192]{0:T(1024)S(1)}, s32[8192]{0:T(1024)}, u32[]{:S(2)}) copy-start(s32[8192]{0:T(1024)} %param.14) | copy-start | bytes 98308
  83.2 143.6 %all-gather.8.cloned.1.call-start = ((), (), s32[]{:S(2)}) async-start(), calls=%async_computation.3 | async-start | bytes 2162688 | tf_op jit(solution)/shard_map/all_gather | solution.py:83
  83.9 264.8 %reduce-scatter.2.cloned.1.call-start = ((), (), s32[]{:S(2)}) async-start(), calls=%async_computation.2 | async-start | bytes 2228224 | tf_op jit(solution)/shard_map/reduce_scatter | solution.py:105
Sparse Core Ops, SparseCore 0:
  10.3 66.3 all-gather.5
  83.3 72.6 all-gather.9
  158.0 68.7 all-gather.7
  262.7 86.0 reduce-scatter.1
where the time goes:
time: 356 us; the launch traced here: 355 us
  waiting for transfers between devices  294 us (83%)
  matrix products  32.7 us (9%)
  between operations  13.3 us (4%)
  other arithmetic  7.89 us (2%)
  local copies, waits for them, and re-layouts  7.14 us (2%)
    reduce_scatter x1, waiting for transfers between devices, on_device(): lax.psum_scatter(partial_value.astype(jnp.bfloat16), 'head', scatter_dime...  86.2 us
    all_gather x1, waiting for transfers between devices, on_device(): lax.all_gather(key_rows, 'seq', axis=0, tiled=True)  70.8 us
    all_gather x1, waiting for transfers between devices, on_device(): lax.all_gather(value_rows, 'seq', axis=0, tiled=True)  70.4 us
    all_gather x1, waiting for transfers between devices, on_device(): gathered = lax.all_gather(tokens, 'head', axis=1, tiled=True)  64.8 us
    dot_general x8, matrix products, absorb(): jnp.einsum('qhd,khd->hqk', queries, block_keys.reshape(key_count, local_h...  14.1 us
    dot_general x8, matrix products, absorb(): jnp.einsum('hqk,khd->hqd', weights.astype(jnp.bfloat16), block_values.res...  13.2 us
  transfers between devices with their start and end apart: 4, of which 4 were waited for; matrix products, arithmetic and copies ran while one was open for 2% of the time, Pallas kernels for 0%

commit v1 on v0

v1 whole, which is shorter than its diff:
```python
import jax
import jax.numpy as jnp
from jax import lax
from jax.experimental import pallas as pl
from jax.experimental.pallas import tpu as pltpu
from jax.sharding import PartitionSpec as P

D = 4096
HD = 128
ROWS = 256
SPAN = 128
BLOCK_Z = 4
MASKED = -1e30
EPSILON = 1e-06
LOG2_E = 1.4426950408889634
SCALE = HD**-0.5 * LOG2_E
PART_ROWS = HD + 16


def project_kernel(x_ref, gain_ref, w_ref, q_ref, kv_ref, inv_ref, acc_ref):
    step = pl.program_id(0)
    blocks = x_ref.shape[0]
    per_step = blocks // pl.num_programs(0)

    @pl.when(step == 0)
    def _():
        total = jnp.zeros((ROWS, x_ref.shape[2]), jnp.float32)
        for j in range(blocks):
            piece = x_ref[j].astype(jnp.float32)
            total = total + piece * piece
        mean = jnp.sum(total, axis=1, keepdims=True) * (1.0 / D)
        inv_ref[...] = jnp.broadcast_to(lax.rsqrt(mean + EPSILON), inv_ref.shape)
        acc_ref[...] = jnp.zeros_like(acc_ref)

    width = x_ref.shape[2]
    inverse = jnp.concatenate([inv_ref[...]] * (width // 128), axis=1)
    sums = acc_ref[...]
    for i in range(per_step):
        piece = x_ref[step * per_step + i].astype(jnp.float32)
        gain = gain_ref[:, i * width : (i + 1) * width]
        normed = (piece * inverse * gain).astype(jnp.bfloat16)
        rows = slice(i * width, (i + 1) * width)
        weights = jnp.concatenate([w_ref[0, rows], w_ref[1, rows], w_ref[2, rows]], axis=1)
        sums = sums + jnp.dot(normed, weights, preferred_element_type=jnp.float32)
    acc_ref[...] = sums

    @pl.when(step == pl.num_programs(0) - 1)
    def _():
        done = sums.astype(jnp.bfloat16)
        q_ref[...] = done[:, :HD]
        kv_ref[...] = done[:, HD:]


def project(x, gain, w):
    blocks, _, width = x.shape
    steps = 4
    depth = D // steps
    return pl.pallas_call(
        project_kernel,
        grid=(steps,),
        in_specs=[
            pl.BlockSpec((blocks, ROWS, width), lambda s: (0, 0, 0)),
            pl.BlockSpec((1, depth), lambda s: (0, s)),
            pl.BlockSpec((3, depth, HD), lambda s: (0, s, 0)),
        ],
        out_specs=[
            pl.BlockSpec((ROWS, HD), lambda s: (0, 0)),
            pl.BlockSpec((ROWS, 2 * HD), lambda s: (0, 0)),
        ],
        out_shape=[
            jax.ShapeDtypeStruct((ROWS, HD), jnp.bfloat16),
            jax.ShapeDtypeStruct((ROWS, 2 * HD), jnp.bfloat16),
        ],
        scratch_shapes=[
            pltpu.VMEM((ROWS, 128), jnp.float32),
            pltpu.VMEM((ROWS, 3 * HD), jnp.float32),
        ],
        name="project",
    )(x, gain, w)


def attend_kernel(q_ref, qcode_ref, kv_ref, kcode_ref, out_ref, vt_ref):
    keys = kv_ref.shape[0] * ROWS

    @pl.when(pl.program_id(0) == 0)
    def _():
        for j in range(kv_ref.shape[0]):
            vt_ref[:, j * ROWS : (j + 1) * ROWS] = jnp.transpose(kv_ref[j][:, HD:])

    key_rows = kv_ref[...].reshape(keys, 2 * HD)[:, :HD]
    raw = lax.dot_general(
        key_rows, q_ref[0], (((1,), (1,)), ((), ())), preferred_element_type=jnp.float32
    )
    qcode = qcode_ref[0]
    kcode = jnp.concatenate([kcode_ref[...]] * (ROWS // 128), axis=1)
    seen = (kcode < (qcode & -8)) | (kcode == qcode)
    scores = jnp.where(seen, raw * SCALE, MASKED)
    best = jnp.max(scores, axis=0, keepdims=True)
    weights = jnp.exp2(scores - best)
    total = jnp.sum(weights, axis=0, keepdims=True)
    mixed = jnp.dot(vt_ref[...], weights.astype(jnp.bfloat16), preferred_element_type=jnp.float32)
    out_ref[0, :HD] = (mixed / total).astype(jnp.bfloat16)
    level = best + jnp.log2(total)
    high = level.astype(jnp.bfloat16).astype(jnp.float32)
    rest = level - high
    middle = rest.astype(jnp.bfloat16).astype(jnp.float32)
    low = rest - middle
    row = lax.broadcasted_iota(jnp.int32, (16, ROWS), 0)
    stats = jnp.where(row == 0, high, jnp.where(row == 1, middle, jnp.where(row == 2, low, 0.0)))
    out_ref[0, HD:] = stats.astype(jnp.bfloat16)


def attend(q, qcode, kv, kcode):
    groups = q.shape[0]
    keys = kv.shape[0] * ROWS
    return pl.pallas_call(
        attend_kernel,
        grid=(groups,),
        in_specs=[
            pl.BlockSpec((1, ROWS, HD), lambda i: (i, 0, 0)),
            pl.BlockSpec((1, 1, ROWS), lambda i: (i, 0, 0)),
            pl.BlockSpec(kv.shape, lambda i: (0, 0, 0)),
            pl.BlockSpec((keys, 128), lambda i: (0, 0)),
        ],
        out_specs=pl.BlockSpec((1, PART_ROWS, ROWS), lambda i: (i, 0, 0)),
        out_shape=jax.ShapeDtypeStruct((groups, PART_ROWS, ROWS), jnp.bfloat16),
        scratch_shapes=[pltpu.VMEM((HD, keys), jnp.bfloat16)],
        name="attend",
    )(q, qcode, kv, kcode)


def combine_kernel(part_ref, out_ref):
    groups = part_ref.shape[0]
    levels = []
    for j in range(groups):
        stats = part_ref[j, HD:].astype(jnp.float32)
        levels.append(stats[0:1] + stats[1:2] + stats[2:3])
    best = levels[0]
    for level in levels[1:]:
        best = jnp.maximum(best, level)
    total = jnp.zeros_like(best)
    mixed = jnp.zeros((HD, ROWS), jnp.float32)
    for j in range(groups):
        share = jnp.exp2(levels[j] - best)
        total = total + share
        mixed = mixed + share * part_ref[j, :HD].astype(jnp.float32)
    out_ref[...] = jnp.transpose(mixed / total).astype(jnp.bfloat16)


def combine(parts):
    return pl.pallas_call(
        combine_kernel,
        out_shape=jax.ShapeDtypeStruct((ROWS, HD), jnp.bfloat16),
        name="combine",
    )(parts)


def output_kernel(attended_ref, w_ref, out_ref):
    total = jnp.zeros(out_ref.shape, jnp.float32)
    for h in range(attended_ref.shape[0]):
        head_out = jnp.dot(attended_ref[h], w_ref[h], preferred_element_type=jnp.float32)
        total = total + head_out.astype(jnp.bfloat16).astype(jnp.float32)
    out_ref[...] = total.astype(jnp.bfloat16)


def output(attended, w):
    return pl.pallas_call(
        output_kernel,
        out_shape=jax.ShapeDtypeStruct((ROWS, w.shape[2]), jnp.bfloat16),
        name="output",
    )(attended, w)


def send_to_all(array, axis, count, groups=None):
    copies = jnp.broadcast_to(array[None], (count,) + array.shape)
    return lax.all_to_all(copies, axis, 0, 0, axis_index_groups=groups)


def make_on_device(n_seq, n_head):
    group = 2 * BLOCK_Z
    near = [[g * group + i for i in range(group)] for g in range(n_seq // group)]
    far = [[g * group + i for g in range(n_seq // group)] for i in range(group)]
    far_count = n_seq // group

    def on_device(tokens, norm_gain, w_qkv, w_out, span_order, frame_id, camera_id):
        columns = tokens.shape[1]
        gathered = send_to_all(tokens, "head", n_head)
        w_split = w_out.reshape(HD, n_head, columns).transpose(1, 0, 2)
        gathered, w_split = lax.optimization_barrier((gathered, w_split))
        w_columns = lax.all_to_all(w_split, "head", 0, 0)

        queries, kv = project(gathered, norm_gain.reshape(1, D), w_qkv.transpose(1, 0, 2))

        code = (frame_id * 8 + camera_id).reshape(-1, SPAN)[span_order]
        code = code.reshape(n_seq // group, group, ROWS)
        place = lax.axis_index("seq")
        query_code = lax.dynamic_index_in_dim(code, place // group, 0, keepdims=False)
        key_code = lax.dynamic_index_in_dim(code, place % group, 1, keepdims=False)
        key_code = jnp.broadcast_to(key_code.reshape(-1, 1), (far_count * ROWS, 128))

        all_queries = lax.all_gather(queries, "seq", axis_index_groups=near)
        all_kv = send_to_all(kv, "seq", far_count, far)
        parts = attend(all_queries, query_code[:, None, :], all_kv, key_code)
        parts = lax.all_to_all(parts, "seq", 0, 0, axis_index_groups=near)
        attended = combine(parts)
        all_attended = send_to_all(attended, "head", n_head)
        return output(all_attended, w_columns)

    return on_device


def solution(mesh):
    placed = (P("seq", "head"), P(), P(None, None, "head"), P("head", None), P(), P(), P())
    return jax.shard_map(
        make_on_device(mesh.shape["seq"], mesh.shape["head"]),
        mesh=mesh,
        in_specs=placed,
        out_specs=P("seq", "head"),
        check_vma=False,
    )
```

time: 356 us -> 171 us (0.48)
  waiting for transfers between devices: 294 us -> 35.9 us
  blocking collectives: 0 us -> 71.9 us
  matrix products: 32.7 us -> 0 us
  starting transfers between devices: 0.12 us -> 31.2 us
  Pallas kernels: 0 us -> 18.8 us
  between operations: 13.3 us -> 0.1 us
  other arithmetic: 7.89 us -> 0.02 us
  local copies, waits for them, and re-layouts: 7.14 us -> 11.8 us
    all_gather x3 -> x0, waiting for transfers between devices: 206 us -> none  [the longest x1 70.8 us: on_device(): lax.all_gather(key_rows, 'seq', axis=0, tiled=True)]
    reduce_scatter x1 -> x0, waiting for transfers between devices: 86.2 us -> none  [on_device(): lax.psum_scatter(partial_value.astype(jnp.bfloat16), 'head', scatter_dime...]
    all_to_all x0 -> x2, blocking collectives: none -> 40.5 us  [the longest x1 20.9 us: on_device(): parts = lax.all_to_all(parts, 'seq', 0, 0, axis_index_groups=near)]
    all_to_all x0 -> x3, waiting for transfers between devices: none -> 35.9 us  [the longest x2 22.5 us: send_to_all(): return lax.all_to_all(copies, axis, 0, 0, axis_index_groups=groups)]
    dot_general x18 -> x0, matrix products: 32.7 us -> none  [the longest x8 14.1 us: absorb(): jnp.einsum('qhd,khd->hqk', queries, block_keys.reshape(key_count, local_h...]
    all_gather x0 -> x1, blocking collectives: none -> 31.4 us  [on_device(): all_queries = lax.all_gather(queries, 'seq', axis_index_groups=near)]
    all_to_all x0 -> x3, starting transfers between devices: none -> 31.2 us  [the longest x2 24.8 us: send_to_all(): return lax.all_to_all(copies, axis, 0, 0, axis_index_groups=groups)]
    pallas_call x0 -> x4, Pallas kernels: none -> 18.8 us  [the longest x1 8.38 us: attend(): pl.pallas_call(attend_kernel, grid=(groups,), in_specs=[pl.BlockSpec((1,...]
  transfers between devices with their start and end apart: 4 -> 3, of which waited for: 4 -> 2; matrix products, arithmetic and copies ran while one was open for 2% -> 2% of each run, Pallas kernels for 0% -> 1%
where the time goes in v1:
time: 171 us; the launch traced here: 170 us
  blocking collectives  71.9 us (42%)
  waiting for transfers between devices  35.9 us (21%)
  starting transfers between devices  31.2 us (18%)
  Pallas kernels  18.8 us (11%)
  local copies, waits for them, and re-layouts  11.8 us (7%)
    all_gather x1, blocking collectives, on_device(): all_queries = lax.all_gather(queries, 'seq', axis_index_groups=near)  31.4 us
    all_to_all x2, starting transfers between devices, send_to_all(): return lax.all_to_all(copies, axis, 0, 0, axis_index_groups=groups)  24.8 us
    all_to_all x2, waiting for transfers between devices, send_to_all(): return lax.all_to_all(copies, axis, 0, 0, axis_index_groups=groups)  22.5 us
    all_to_all x1, blocking collectives, on_device(): parts = lax.all_to_all(parts, 'seq', 0, 0, axis_index_groups=near)  20.9 us
    all_to_all x1, blocking collectives, send_to_all(): return lax.all_to_all(copies, axis, 0, 0, axis_index_groups=groups)  19.6 us
    all_to_all x1, waiting for transfers between devices, on_device(): w_columns = lax.all_to_all(w_split, 'head', 0, 0)  13.4 us
    pallas_call x1, Pallas kernels, attend(): pl.pallas_call(attend_kernel, grid=(groups,), in_specs=[pl.BlockSpec((1,...  8.38 us
    all_to_all x1, starting transfers between devices, on_device(): w_columns = lax.all_to_all(w_split, 'head', 0, 0)  6.42 us
  transfers between devices with their start and end apart: 3, of which 2 were waited for; matrix products, arithmetic and copies ran while one was open for 2% of the time, Pallas kernels for 1%

profile of v1, /device:TPU:6, one launch (start us, length us, event | category | flops | bytes accessed | tf_op | source)
XLA Modules:
  0.0 169.7 jit_solution(7929258913829125817)
XLA Ops:
  0.0 2.4 %broadcast_in_dim.14 = bf16[16,256,256]{2,1,0:T(8,128)(2,1)} broadcast(bf16[256,256]{1,0:T(8,128)(2,1)} %param.7), dimensions={1,2} | broadcast | bytes 2228224 | tf_op jit(solution)/shard_map/broadcast_in_dim | solution.py:175
  2.4 9.4 %all-to-all-start = ((bf16[16,256,256]{2,1,0:T(8,128)(2,1)}), bf16[16,256,256]{2,1,0:T(8,128)(2,1)S(1)}, u32[]{:S(2)}, u32[]{:S(2)}) async-start(bf16[16,256,256]{2,1,0:T(8,128)(2,1)} %broadcast_in_dim.14), calls=%async_computation | async-start | bytes 4194304 | tf_op jit(solution)/shard_map/all_to_all | solution.py:176
  11.8 1.6 copy.9
  13.5 1.3 copy.10
  14.8 22.5 %all-to-all-done.x_ref = bf16[16,256,256]{2,1,0:T(8,128)(2,1)S(1)} async-done(((bf16[16,256,256]{2,1,0:T(8,128)(2,1)}), bf16[16,256,256]{2,1,0:T(8,128)(2,1)S(1)}, u32[]{:S(2)}, u32[]{:S(2)}) %all-to-all-start) | async-done | bytes 2097184 | tf_op jit(solution)/shard_map/all_to_all | solution.py:176
  37.3 1.3 copy-done
  38.6 5.6 %project.1 = (bf16[256,128]{1,0:T(8,128)(2,1)}, bf16[256,256]{1,0:T(8,128)(2,1)}) custom-call(bf16[16,256,256]{2,1,0:T(8,128)(2,1)} %copy-done, f32[1,4096]{1,0:T(1,128)} %bitcast.15, bf16[3,4096,128]{2,1,0:T(8,128)(2,1)} %bitcast.12), custom_call_target="tpu_custom_call" | custom-call | tf_op jit(solution)/shard_map/project/pallas_call | solution.py:58
  44.2 1.8 %broadcast_in_dim.34 = bf16[4,256,256]{2,1,0:T(8,128)(2,1)} broadcast(bf16[256,256]{1,0:T(8,128)(2,1)} %get-tuple-element.11), dimensions={1,2} | broadcast | bytes 655360 | tf_op jit(solution)/shard_map/broadcast_in_dim | solution.py:175
  46.0 15.3 %all-to-all-start.1 = ((bf16[4,256,256]{2,1,0:T(8,128)(2,1)}), bf16[4,256,256]{2,1,0:T(8,128)(2,1)S(1)}, u32[]{:S(2)}, u32[]{:S(2)}) async-start(bf16[4,256,256]{2,1,0:T(8,128)(2,1)} %broadcast_in_dim.34), calls=%async_computation.1 | async-start | bytes 1048576 | tf_op jit(solution)/shard_map/all_to_all | solution.py:176
  61.3 0.0 copy-done.6
  61.4 0.6 gather_fusion
  62.0 0.6 copy.14
  62.6 31.4 %all-gather = bf16[2048,128]{1,0:T(8,128)(2,1)} all-gather(bf16[256,128]{1,0:T(8,128)(2,1)S(1)} %copy-done.3), channel_id=2, replica_groups={{0,16,32,48,64,80,96,112},{128,144,160,176,192,208,224,240},{256,272,28..., dimensions={0}, use_global_device_ids=true | all-gather | bytes 589824 | tf_op jit(solution)/shard_map/all_gather | solution.py:201
  94.0 0.0 all-to-all-done.1.kv_ref
  94.0 1.0 broadcast_in_dim.36.kcode_ref
  95.0 0.0 copy-done.2
  95.0 8.4 %attend.1 = bf16[8,144,256]{2,1,0:T(8,128)(2,1)} custom-call(bf16[8,256,128]{2,1,0:T(8,128)(2,1)} %bitcast.13, s32[8,1,256]{2,1,0:T(1,128)} %bitcast.14, bf16[4,256,256]{2,1,0:T(8,128)(2,1)} %copy-done.2, s32[1024,128]{1,0:T(8,128)} %broadcast_in_dim.36.kcode_ref), custom_call_target="tpu_custom_call" | custom-call | tf_op jit(solution)/shard_map/attend/pallas_call | solution.py:116
  103.4 20.9 %all_to_all.25.part_ref = bf16[8,144,256]{2,1,0:T(8,128)(2,1)} all-to-all(bf16[8,144,256]{2,1,0:T(8,128)(2,1)} %attend.1), channel_id=1, replica_groups={{0,16,32,48,64,80,96,112},{128,144,160,176,192,208,224,240},{256,272,28..., dimensions={0} | all-to-all | bytes 1179648 | tf_op jit(solution)/shard_map/all_to_all | solution.py:204
  124.3 6.4 %all-to-all-start.4 = ((bf16[16,128,256]{2,1,0:T(8,128)(2,1)}), bf16[16,128,256]{2,1,0:T(8,128)(2,1)S(1)}, u32[]{:S(2)}, u32[]{:S(2)}) async-start(bf16[16,128,256]{2,1,0:T(8,128)(2,1)} %bitcast.1), calls=%async_computation.4 | async-start | bytes 2097152 | tf_op jit(solution)/shard_map/all_to_all | solution.py:190
  130.8 1.9 %combine.1 = bf16[256,128]{1,0:T(8,128)(2,1)} custom-call(bf16[8,144,256]{2,1,0:T(8,128)(2,1)} %all_to_all.25.part_ref), custom_call_target="tpu_custom_call" | custom-call | tf_op jit(solution)/shard_map/combine/pallas_call | solution.py:151
  132.6 13.4 %all-to-all-done.4.w_ref = bf16[16,128,256]{2,1,0:T(8,128)(2,1)S(1)} async-done(((bf16[16,128,256]{2,1,0:T(8,128)(2,1)}), bf16[16,128,256]{2,1,0:T(8,128)(2,1)S(1)}, u32[]{:S(2)}, u32[]{:S(2)}) %all-to-all-start.4) | async-done | bytes 1048608 | tf_op jit(solution)/shard_map/all_to_all | solution.py:190
  146.1 1.1 broadcast_in_dim.37
  147.2 19.6 %all_to_all.26.attended_ref = bf16[16,256,128]{2,1,0:T(8,128)(2,1)} all-to-all(bf16[16,256,128]{2,1,0:T(8,128)(2,1)S(1)} %broadcast_in_dim.37), channel_id=1, replica_groups=mesh['seq'=32,'head'=16] {'head'}, dimensions={0} | all-to-all | bytes 2097152 | tf_op jit(solution)/shard_map/all_to_all | solution.py:176
  166.8 2.9 %output.1 = bf16[256,256]{1,0:T(8,128)(2,1)} custom-call(bf16[16,256,128]{2,1,0:T(8,128)(2,1)} %all_to_all.26.attended_ref, bf16[16,128,256]{2,1,0:T(8,128)(2,1)} %copy-done.1), custom_call_target="tpu_custom_call" | custom-call | tf_op jit(solution)/shard_map/output/pallas_call | solution.py:167
  (17 shorter events, 0.1 us)
Async XLA Ops:
  2.4 34.9 %all-to-all-start = ((bf16[16,256,256]{2,1,0:T(8,128)(2,1)}), bf16[16,256,256]{2,1,0:T(8,128)(2,1)S(1)}, u32[]{:S(2)}, u32[]{:S(2)}) async-start(bf16[16,256,256]{2,1,0:T(8,128)(2,1)} %broadcast_in_dim.14), calls=%async_computation | async-start | bytes 4194304 | tf_op jit(solution)/shard_map/all_to_all | solution.py:176
  37.3 1.3 copy-start
  38.6 22.7 %copy-start.6 = (s32[64]{0:T(128)S(1)}, s32[64]{0:T(128)}, u32[]{:S(2)}) copy-start(s32[64]{0:T(128)} %param.11) | copy-start | bytes 772
  38.6 22.7 %copy-start.4 = (s32[8192]{0:T(1024)S(1)}, s32[8192]{0:T(1024)}, u32[]{:S(2)}) copy-start(s32[8192]{0:T(1024)} %param.13) | copy-start | bytes 98308
  38.6 22.7 %copy-start.5 = (s32[8192]{0:T(1024)S(1)}, s32[8192]{0:T(1024)}, u32[]{:S(2)}) copy-start(s32[8192]{0:T(1024)} %param.12) | copy-start | bytes 98308
  44.2 18.4 %copy-start.3 = (bf16[256,128]{1,0:T(8,128)(2,1)S(1)}, bf16[256,128]{1,0:T(8,128)(2,1)}, u32[]{:S(2)}) copy-start(bf16[256,128]{1,0:T(8,128)(2,1)} %get-tuple-element.10) | copy-start | bytes 196612
  46.0 48.0 %all-to-all-start.1 = ((bf16[4,256,256]{2,1,0:T(8,128)(2,1)}), bf16[4,256,256]{2,1,0:T(8,128)(2,1)S(1)}, u32[]{:S(2)}, u32[]{:S(2)}) async-start(bf16[4,256,256]{2,1,0:T(8,128)(2,1)} %broadcast_in_dim.34), calls=%async_computation.1 | async-start | bytes 1048576 | tf_op jit(solution)/shard_map/all_to_all | solution.py:176
  94.0 1.0 copy-start.2
  124.3 21.7 %all-to-all-start.4 = ((bf16[16,128,256]{2,1,0:T(8,128)(2,1)}), bf16[16,128,256]{2,1,0:T(8,128)(2,1)S(1)}, u32[]{:S(2)}, u32[]{:S(2)}) async-start(bf16[16,128,256]{2,1,0:T(8,128)(2,1)} %bitcast.1), calls=%async_computation.4 | async-start | bytes 2097152 | tf_op jit(solution)/shard_map/all_to_all | solution.py:190
  146.1 20.7 %copy-start.1 = (bf16[16,128,256]{2,1,0:T(8,128)(2,1)}, bf16[16,128,256]{2,1,0:T(8,128)(2,1)S(1)}, u32[]{:S(2)}) copy-start(bf16[16,128,256]{2,1,0:T(8,128)(2,1)S(1)} %all-to-all-done.4.w_ref) | copy-start | bytes 3145732

commit v2 on v1

--- a/solution.py
+++ b/solution.py
@@ -5,11 +5,14 @@
 from jax.experimental.pallas import tpu as pltpu
 from jax.sharding import PartitionSpec as P
 
+
 D = 4096
 HD = 128
 ROWS = 256
 SPAN = 128
+CORES = 2
 BLOCK_Z = 4
+GRANT = 16 << 20
 MASKED = -1e30
 EPSILON = 1e-06
 LOG2_E = 1.4426950408889634
@@ -75,26 +78,39 @@
             pltpu.VMEM((ROWS, 128), jnp.float32),
             pltpu.VMEM((ROWS, 3 * HD), jnp.float32),
         ],
+        compiler_params=pltpu.CompilerParams(vmem_limit_bytes=GRANT),
         name="project",
     )(x, gain, w)
 
 
-def attend_kernel(q_ref, qcode_ref, kv_ref, kcode_ref, out_ref, vt_ref):
-    keys = kv_ref.shape[0] * ROWS
+def attend_kernel(q_ref, qcode_ref, own_ref, other_ref, kcode_ref, out_ref, vt_ref):
+    count = own_ref.shape[0]
 
     @pl.when(pl.program_id(0) == 0)
     def _():
-        for j in range(kv_ref.shape[0]):
-            vt_ref[:, j * ROWS : (j + 1) * ROWS] = jnp.transpose(kv_ref[j][:, HD:])
-
-    key_rows = kv_ref[...].reshape(keys, 2 * HD)[:, :HD]
-    raw = lax.dot_general(
-        key_rows, q_ref[0], (((1,), (1,)), ((), ())), preferred_element_type=jnp.float32
-    )
+        for part, ref in enumerate((own_ref, other_ref)):
+            for j in range(count):
+                at = (part * count + j) * ROWS
+                vt_ref[:, at : at + ROWS] = jnp.transpose(ref[j][:, HD:])
+
     qcode = qcode_ref[0]
-    kcode = jnp.concatenate([kcode_ref[...]] * (ROWS // 128), axis=1)
-    seen = (kcode < (qcode & -8)) | (kcode == qcode)
-    scores = jnp.where(seen, raw * SCALE, MASKED)
+    qbase = qcode & -8
+    queries = q_ref[0]
+    scores = []
+    for part, ref in enumerate((own_ref, other_ref)):
+        for j in range(count):
+            at = (part * count + j) * ROWS
+            raw = lax.dot_general(
+                ref[j][:, :HD],
+                queries,
+                (((1,), (1,)), ((), ())),
+                preferred_element_type=jnp.float32,
+            )
+            code = kcode_ref[at : at + ROWS, :]
+            kcode = jnp.concatenate([code] * (ROWS // 128), axis=1)
+            seen = (kcode < qbase) | (kcode == qcode)
+            scores.append(jnp.where(seen, raw * SCALE, MASKED))
+    scores = jnp.concatenate(scores, axis=0)
     best = jnp.max(scores, axis=0, keepdims=True)
     weights = jnp.exp2(scores - best)
     total = jnp.sum(weights, axis=0, keepdims=True)
@@ -110,23 +126,25 @@
     out_ref[0, HD:] = stats.astype(jnp.bfloat16)
 
 
-def attend(q, qcode, kv, kcode):
+def attend(q, qcode, own_kv, other_kv, kcode):
     groups = q.shape[0]
-    keys = kv.shape[0] * ROWS
+    keys = kcode.shape[0]
     return pl.pallas_call(
         attend_kernel,
         grid=(groups,),
         in_specs=[
             pl.BlockSpec((1, ROWS, HD), lambda i: (i, 0, 0)),
             pl.BlockSpec((1, 1, ROWS), lambda i: (i, 0, 0)),
-            pl.BlockSpec(kv.shape, lambda i: (0, 0, 0)),
+            pl.BlockSpec(own_kv.shape, lambda i: (0, 0, 0)),
+            pl.BlockSpec(other_kv.shape, lambda i: (0, 0, 0)),
             pl.BlockSpec((keys, 128), lambda i: (0, 0)),
         ],
         out_specs=pl.BlockSpec((1, PART_ROWS, ROWS), lambda i: (i, 0, 0)),
         out_shape=jax.ShapeDtypeStruct((groups, PART_ROWS, ROWS), jnp.bfloat16),
         scratch_shapes=[pltpu.VMEM((HD, keys), jnp.bfloat16)],
+        compiler_params=pltpu.CompilerParams(vmem_limit_bytes=GRANT),
         name="attend",
-    )(q, qcode, kv, kcode)
+    )(q, qcode, own_kv, other_kv, kcode)
 
 
 def combine_kernel(part_ref, out_ref):
@@ -151,6 +169,7 @@
     return pl.pallas_call(
         combine_kernel,
         out_shape=jax.ShapeDtypeStruct((ROWS, HD), jnp.bfloat16),
+        compiler_params=pltpu.CompilerParams(vmem_limit_bytes=GRANT),
         name="combine",
     )(parts)
 
@@ -167,6 +186,7 @@
     return pl.pallas_call(
         output_kernel,
         out_shape=jax.ShapeDtypeStruct((ROWS, w.shape[2]), jnp.bfloat16),
+        compiler_params=pltpu.CompilerParams(vmem_limit_bytes=GRANT),
         name="output",
     )(attended, w)
 
@@ -177,30 +197,43 @@
 
 
 def make_on_device(n_seq, n_head):
-    group = 2 * BLOCK_Z
-    near = [[g * group + i for i in range(group)] for g in range(n_seq // group)]
-    far = [[g * group + i for g in range(n_seq // group)] for i in range(group)]
-    far_count = n_seq // group
+    group = CORES * BLOCK_Z
+    blocks = n_seq // group
+    near = [
+        [g * group + b * CORES + c for b in range(BLOCK_Z)] for g in range(blocks) for c in range(CORES)
+    ]
+    far = [[g * group + i for g in range(blocks)] for i in range(group)]
+    swap = [(i, i ^ 1) for i in range(n_seq)]
+    keys = CORES * blocks * ROWS
+
+    def codes(span_order, frame_id, camera_id):
+        code = (frame_id * 8 + camera_id).reshape(-1, SPAN)[span_order]
+        code = code.reshape(blocks, BLOCK_Z, CORES, ROWS)
+        place = lax.axis_index("seq")
+        core = place % CORES
+        query_code = lax.dynamic_index_in_dim(code, place // group, 0, keepdims=False)
+        query_code = lax.dynamic_index_in_dim(query_code, core, 1, keepdims=False)
+        key_code = lax.dynamic_index_in_dim(code, place // CORES % BLOCK_Z, 1, keepdims=False)
+        own = lax.dynamic_index_in_dim(key_code, core, 1, keepdims=False)
+        other = lax.dynamic_index_in_dim(key_code, 1 - core, 1, keepdims=False)
+        key_code = jnp.concatenate([own, other]).reshape(-1, 1)
+        return query_code[:, None, :], jnp.broadcast_to(key_code, (keys, 128))
 
     def on_device(tokens, norm_gain, w_qkv, w_out, span_order, frame_id, camera_id):
         columns = tokens.shape[1]
         gathered = send_to_all(tokens, "head", n_head)
+        query_code, key_code = codes(span_order, frame_id, camera_id)
         w_split = w_out.reshape(HD, n_head, columns).transpose(1, 0, 2)
-        gathered, w_split = lax.optimization_barrier((gathered, w_split))
+        gathered, w_split, query_code, key_code = lax.optimization_barrier(
+            (gathered, w_split, query_code, key_code)
+        )
         w_columns = lax.all_to_all(w_split, "head", 0, 0)
-
         queries, kv = project(gathered, norm_gain.reshape(1, D), w_qkv.transpose(1, 0, 2))
-
-        code = (frame_id * 8 + camera_id).reshape(-1, SPAN)[span_order]
-        code = code.reshape(n_seq // group, group, ROWS)
-        place = lax.axis_index("seq")
-        query_code = lax.dynamic_index_in_dim(code, place // group, 0, keepdims=False)
-        key_code = lax.dynamic_index_in_dim(code, place % group, 1, keepdims=False)
-        key_code = jnp.broadcast_to(key_code.reshape(-1, 1), (far_count * ROWS, 128))
-
         all_queries = lax.all_gather(queries, "seq", axis_index_groups=near)
-        all_kv = send_to_all(kv, "seq", far_count, far)
-        parts = attend(all_queries, query_code[:, None, :], all_kv, key_code)
+        all_queries, kv, w_columns = lax.optimization_barrier((all_queries, kv, w_columns))
+        own_kv = send_to_all(kv, "seq", blocks, far)
+        other_kv = lax.ppermute(own_kv, "seq", swap)
+        parts = attend(all_queries, query_code, own_kv, other_kv, key_code)
         parts = lax.all_to_all(parts, "seq", 0, 0, axis_index_groups=near)
         attended = combine(parts)
         all_attended = send_to_all(attended, "head", n_head)

time: 171 us -> 148 us (0.87)
  blocking collectives: 71.9 us -> 87.7 us
  starting transfers between devices: 31.2 us -> 17.5 us
  waiting for transfers between devices: 35.9 us -> 23.5 us
  Pallas kernels: 18.8 us -> 8.92 us
  local copies, waits for them, and re-layouts: 11.8 us -> 9.49 us
    all_to_all x1 -> x2, blocking collectives: 19.6 us -> 58.5 us  [send_to_all(): return lax.all_to_all(copies, axis, 0, 0, axis_index_groups=groups)]
    all_gather x1, blocking collectives: 31.4 us -> 15.5 us  [on_device(): all_queries = lax.all_gather(queries, 'seq', axis_index_groups=near)]
    all_to_all x2 -> x1, starting transfers between devices: 24.8 us -> 9.4 us  [send_to_all(): return lax.all_to_all(copies, axis, 0, 0, axis_index_groups=groups)]
    all_to_all x1, waiting for transfers between devices: 13.4 us -> 0.01 us  [on_device(): w_columns = lax.all_to_all(w_split, 'head', 0, 0)]
    all_to_all x1, blocking collectives: 20.9 us -> 13.7 us  [on_device(): parts = lax.all_to_all(parts, 'seq', 0, 0, axis_index_groups=near)]
    pallas_call x1, Pallas kernels: 8.38 us -> 4.95 us  [attend(): pl.pallas_call(attend_kernel, grid=(groups,), in_specs=[pl.BlockSpec((1,...]
    pallas_call x1, Pallas kernels: 5.58 us -> 2.47 us  [project(): pl.pallas_call(project_kernel, grid=(steps,), in_specs=[pl.BlockSpec((blo...]
    broadcast_in_dim x3, local copies, waits for them, and re-layouts: 5.28 us -> 2.66 us  [send_to_all(): copies = jnp.broadcast_to(array[None], (count,) + array.shape)]
  transfers between devices with their start and end apart: 3 -> 3, of which waited for: 2 -> 2; matrix products, arithmetic and copies ran while one was open for 2% -> 2% of each run, Pallas kernels for 1% -> 2%
where the time goes in v2:
time: 148 us; the launch traced here: 147 us
  blocking collectives  87.7 us (59%)
  waiting for transfers between devices  23.5 us (16%)
  starting transfers between devices  17.5 us (12%)
  local copies, waits for them, and re-layouts  9.49 us (6%)
  Pallas kernels  8.92 us (6%)
    all_to_all x2, blocking collectives, send_to_all(): return lax.all_to_all(copies, axis, 0, 0, axis_index_groups=groups)  58.5 us
    all_to_all x1, waiting for transfers between devices, send_to_all(): return lax.all_to_all(copies, axis, 0, 0, axis_index_groups=groups)  21.7 us
    all_gather x1, blocking collectives, on_device(): all_queries = lax.all_gather(queries, 'seq', axis_index_groups=near)  15.5 us
    all_to_all x1, blocking collectives, on_device(): parts = lax.all_to_all(parts, 'seq', 0, 0, axis_index_groups=near)  13.7 us
    all_to_all x1, starting transfers between devices, send_to_all(): return lax.all_to_all(copies, axis, 0, 0, axis_index_groups=groups)  9.4 us
    all_to_all x1, starting transfers between devices, on_device(): w_columns = lax.all_to_all(w_split, 'head', 0, 0)  6.22 us
    pallas_call x1, Pallas kernels, attend(): pl.pallas_call(attend_kernel, grid=(groups,), in_specs=[pl.BlockSpec((1,...  4.95 us
    unnamed x15, local copies, waits for them, and re-layouts  3.55 us
  transfers between devices with their start and end apart: 3, of which 2 were waited for; matrix products, arithmetic and copies ran while one was open for 2% of the time, Pallas kernels for 2%

profile of v2, /device:TPU:6, one launch (start us, length us, event | category | flops | bytes accessed | tf_op | source)
XLA Modules:
  0.0 147.4 jit_solution(13125956196237260527)
XLA Ops:
  0.0 2.4 %broadcast_in_dim.12 = bf16[16,256,256]{2,1,0:T(8,128)(2,1)} broadcast(bf16[256,256]{1,0:T(8,128)(2,1)} %param.7), dimensions={1,2} | broadcast | bytes 2228224 | tf_op jit(solution)/shard_map/broadcast_in_dim | solution.py:195
  2.4 9.4 %all-to-all-start = ((bf16[16,256,256]{2,1,0:T(8,128)(2,1)}), bf16[16,256,256]{2,1,0:T(8,128)(2,1)S(1)}, u32[]{:S(2)}, u32[]{:S(2)}) async-start(bf16[16,256,256]{2,1,0:T(8,128)(2,1)} %broadcast_in_dim.12), calls=%async_computation | async-start | bytes 4194304 | tf_op jit(solution)/shard_map/all_to_all | solution.py:196
  11.8 0.0 copy-start.3
  11.9 0.0 copy-start.4
  11.9 1.6 %copy.8 = bf16[128,4096]{0,1:T(8,128)(2,1)S(1)} copy(bf16[128,4096]{1,0:T(8,128)(2,1)} %param.10) | data formatting | bytes 2097152 | tf_op args[3]
  13.5 1.3 copy.9
  14.9 0.6 gather_fusion
  15.6 21.7 %all-to-all-done.x_ref = bf16[16,256,256]{2,1,0:T(8,128)(2,1)S(1)} async-done(((bf16[16,256,256]{2,1,0:T(8,128)(2,1)}), bf16[16,256,256]{2,1,0:T(8,128)(2,1)S(1)}, u32[]{:S(2)}, u32[]{:S(2)}) %all-to-all-start) | async-done | bytes 2097184 | tf_op jit(solution)/shard_map/all_to_all | solution.py:196
  37.3 1.3 broadcast_in_dim.15.kcode_ref
  38.6 6.2 %all-to-all-start.1 = ((bf16[16,128,256]{2,1,0:T(8,128)(2,1)}), bf16[16,128,256]{2,1,0:T(8,128)(2,1)S(1)}, u32[]{:S(2)}, u32[]{:S(2)}) async-start(bf16[16,128,256]{2,1,0:T(8,128)(2,1)} %bitcast.19), calls=%async_computation.1 | async-start | bytes 2097152 | tf_op jit(solution)/shard_map/all_to_all | solution.py:230
  44.8 0.0 copy-start.1
  44.8 1.9 %copy-done.1 = bf16[4096,3,128]{2,0,1:T(8,128)(2,1)S(1)} copy-done((bf16[4096,3,128]{2,0,1:T(8,128)(2,1)S(1)}, bf16[4096,3,128]{2,0,1:T(8,128)(2,1)}, u32[]{:S(2)}) %copy-start.1) | copy-done | bytes 3145752
  46.7 2.5 %project.1 = (bf16[256,128]{1,0:T(8,128)(2,1)S(1)}, bf16[256,256]{1,0:T(8,128)(2,1)S(1)}) custom-call(bf16[16,256,256]{2,1,0:T(8,128)(2,1)S(1)} %all-to-all-done.x_ref, f32[1,4096]{1,0:T(1,128)S(1)} %bitcast.18, bf16[3,4096,128]{2,1,0:T(8,128)(2,1)S(1)} %bitcast.16), custom_call_target="tpu_custom_call" | custom-call | tf_op jit(solution)/shard_map/project/pallas_call | solution.py:61
  49.2 15.5 %all-gather = bf16[1024,128]{1,0:T(8,128)(2,1)S(1)} all-gather(bf16[256,128]{1,0:T(8,128)(2,1)S(1)} %get-tuple-element.15), channel_id=2, replica_groups={{0,32,64,96},{16,48,80,112},{128,160,192,224},{144,176,208,240},{256,28..., dimensions={0}, use_global_device_ids=true | all-gather | bytes 327680 | tf_op jit(solution)/shard_map/all_gather | solution.py:232
  64.7 0.0 all-to-all-done.1.w_ref
  64.8 37.6 %all_to_all.25.own_ref = bf16[4,256,256]{2,1,0:T(8,128)(2,1)S(1)} all-to-all(bf16[4,256,256]{2,1,0:T(8,128)(2,1)S(1)} %broadcast_in_dim.16), channel_id=1, replica_groups={{0,128,256,384},{16,144,272,400},{32,160,288,416},{48,176,304,432},{64,..., dimensions={0} | all-to-all | bytes 1048576 | tf_op jit(solution)/shard_map/all_to_all | solution.py:196
  102.4 1.9 %collective-permute-start = (bf16[4,256,256]{2,1,0:T(8,128)(2,1)S(1)}, bf16[4,256,256]{2,1,0:T(8,128)(2,1)S(1)}, u32[]{:S(2)}, u32[]{:S(2)}) collective-permute-start(bf16[4,256,256]{2,1,0:T(8,128)(2,1)S(1)} %all_to_all.25.own_ref), channel_id=1, source_target_pairs={{0,16},{16,0},{32,48},{48,32},{64,80},{80,64},{96,112},{112,96},{1... | collective-permute-start | bytes 1572872 | tf_op jit(solution)/shard_map/ppermute | solution.py:235
  104.3 1.9 %collective-permute-done.other_ref = bf16[4,256,256]{2,1,0:T(8,128)(2,1)S(1)} collective-permute-done((bf16[4,256,256]{2,1,0:T(8,128)(2,1)S(1)}, bf16[4,256,256]{2,1,0:T(8,128)(2,1)S(1)}, u32[]{:S(2)}, u32[]{:S(2)}) %collective-permute-start) | collective-permute-done | bytes 524320 | tf_op jit(solution)/shard_map/ppermute | solution.py:235
  106.2 4.9 %attend.1 = bf16[4,144,256]{2,1,0:T(8,128)(2,1)S(1)} custom-call(bf16[4,256,128]{2,1,0:T(8,128)(2,1)S(1)} %bitcast.17, s32[4,1,256]{2,1,0:T(1,128)S(1)} %dynamic-slice_bitcast_fusion.qcode_ref, bf16[4,256,256]{2,1,0:T(8,128)(2,1)S(1)} %all_to_all.25.own_ref, bf16[4,256,256]{2,1,0:T(8,128)(2,1)S(1)} %collective-permute-done.other_ref, s32[2048,128]{1,0:T(8,128)S(1)} %copy-done), custom_call_target="tpu_custom_call" | custom-call | tf_op jit(solution)/shard_map/attend/pallas_call | solution.py:132
  111.1 13.7 %all_to_all.26.part_ref = bf16[4,144,256]{2,1,0:T(8,128)(2,1)S(1)} all-to-all(bf16[4,144,256]{2,1,0:T(8,128)(2,1)S(1)} %attend.1), channel_id=1, replica_groups={{0,32,64,96},{16,48,80,112},{128,160,192,224},{144,176,208,240},{256,28..., dimensions={0} | all-to-all | bytes 589824 | tf_op jit(solution)/shard_map/all_to_all | solution.py:237
  124.8 0.1 combine.1
  125.0 0.2 broadcast_in_dim.34
  125.2 20.9 %all_to_all.27.attended_ref = bf16[16,256,128]{2,1,0:T(8,128)(2,1)S(1)} all-to-all(bf16[16,256,128]{2,1,0:T(8,128)(2,1)S(1)} %broadcast_in_dim.34), channel_id=1, replica_groups=mesh['seq'=32,'head'=16] {'head'}, dimensions={0} | all-to-all | bytes 2097152 | tf_op jit(solution)/shard_map/all_to_all | solution.py:196
  146.0 1.4 output.1
  (18 shorter events, 0.1 us)
Async XLA Ops:
  2.4 34.9 %all-to-all-start = ((bf16[16,256,256]{2,1,0:T(8,128)(2,1)}), bf16[16,256,256]{2,1,0:T(8,128)(2,1)S(1)}, u32[]{:S(2)}, u32[]{:S(2)}) async-start(bf16[16,256,256]{2,1,0:T(8,128)(2,1)} %broadcast_in_dim.12), calls=%async_computation | async-start | bytes 4194304 | tf_op jit(solution)/shard_map/all_to_all | solution.py:196
  11.8 3.0 %copy-start.5 = (s32[64]{0:T(128)S(1)}, s32[64]{0:T(128)}, u32[]{:S(2)}) copy-start(s32[64]{0:T(128)} %param.11) | copy-start | bytes 772
  11.8 3.0 %copy-start.3 = (s32[8192]{0:T(1024)S(1)}, s32[8192]{0:T(1024)}, u32[]{:S(2)}) copy-start(s32[8192]{0:T(1024)} %param.13) | copy-start | bytes 98308
  11.9 3.0 %copy-start.4 = (s32[8192]{0:T(1024)S(1)}, s32[8192]{0:T(1024)}, u32[]{:S(2)}) copy-start(s32[8192]{0:T(1024)} %param.12) | copy-start | bytes 98308
  14.8 30.0 %copy-start.2 = (f32[4096]{0:T(1024)S(1)}, f32[4096]{0:T(1024)}, u32[]{:S(2)}) copy-start(f32[4096]{0:T(1024)} %param.8) | copy-start | bytes 49156
  38.6 26.1 %all-to-all-start.1 = ((bf16[16,128,256]{2,1,0:T(8,128)(2,1)}), bf16[16,128,256]{2,1,0:T(8,128)(2,1)S(1)}, u32[]{:S(2)}, u32[]{:S(2)}) async-start(bf16[16,128,256]{2,1,0:T(8,128)(2,1)} %bitcast.19), calls=%async_computation.1 | async-start | bytes 2097152 | tf_op jit(solution)/shard_map/all_to_all | solution.py:230
  44.8 1.9 %copy-start.1 = (bf16[4096,3,128]{2,0,1:T(8,128)(2,1)S(1)}, bf16[4096,3,128]{2,0,1:T(8,128)(2,1)}, u32[]{:S(2)}) copy-start(bf16[4096,3,128]{2,0,1:T(8,128)(2,1)} %param.9) | copy-start | bytes 9437188
  49.2 57.0 %copy-start = (s32[2048,128]{1,0:T(8,128)S(1)}, s32[2048,128]{1,0:T(8,128)}, u32[]{:S(2)}) copy-start(s32[2048,128]{1,0:T(8,128)} %broadcast_in_dim.15.kcode_ref) | copy-start | bytes 3145732
  102.4 3.8 %collective-permute-start = (bf16[4,256,256]{2,1,0:T(8,128)(2,1)S(1)}, bf16[4,256,256]{2,1,0:T(8,128)(2,1)S(1)}, u32[]{:S(2)}, u32[]{:S(2)}) collective-permute-start(bf16[4,256,256]{2,1,0:T(8,128)(2,1)S(1)} %all_to_all.25.own_ref), channel_id=1, source_target_pairs={{0,16},{16,0},{32,48},{48,32},{64,80},{80,64},{96,112},{112,96},{1... | collective-permute-start | bytes 1572872 | tf_op jit(solution)/shard_map/ppermute | solution.py:235

commit v3 on v2

--- a/solution.py
+++ b/solution.py
@@ -51,10 +51,11 @@
     def _():
         done = sums.astype(jnp.bfloat16)
         q_ref[...] = done[:, :HD]
-        kv_ref[...] = done[:, HD:]
-
-
-def project(x, gain, w):
+        for j in range(kv_ref.shape[0]):
+            kv_ref[j] = done[:, HD:]
+
+
+def project(x, gain, w, copies):
     blocks, _, width = x.shape
     steps = 4
     depth = D // steps
@@ -68,11 +69,11 @@
         ],
         out_specs=[
             pl.BlockSpec((ROWS, HD), lambda s: (0, 0)),
-            pl.BlockSpec((ROWS, 2 * HD), lambda s: (0, 0)),
+            pl.BlockSpec((copies, ROWS, 2 * HD), lambda s: (0, 0, 0)),
         ],
         out_shape=[
             jax.ShapeDtypeStruct((ROWS, HD), jnp.bfloat16),
-            jax.ShapeDtypeStruct((ROWS, 2 * HD), jnp.bfloat16),
+            jax.ShapeDtypeStruct((copies, ROWS, 2 * HD), jnp.bfloat16),
         ],
         scratch_shapes=[
             pltpu.VMEM((ROWS, 128), jnp.float32),
@@ -162,13 +163,15 @@
         share = jnp.exp2(levels[j] - best)
         total = total + share
         mixed = mixed + share * part_ref[j, :HD].astype(jnp.float32)
-    out_ref[...] = jnp.transpose(mixed / total).astype(jnp.bfloat16)
-
-
-def combine(parts):
+    attended = jnp.transpose(mixed / total).astype(jnp.bfloat16)
+    for j in range(out_ref.shape[0]):
+        out_ref[j] = attended
+
+
+def combine(parts, copies):
     return pl.pallas_call(
         combine_kernel,
-        out_shape=jax.ShapeDtypeStruct((ROWS, HD), jnp.bfloat16),
+        out_shape=jax.ShapeDtypeStruct((copies, ROWS, HD), jnp.bfloat16),
         compiler_params=pltpu.CompilerParams(vmem_limit_bytes=GRANT),
         name="combine",
     )(parts)
@@ -189,11 +192,6 @@
         compiler_params=pltpu.CompilerParams(vmem_limit_bytes=GRANT),
         name="output",
     )(attended, w)
-
-
-def send_to_all(array, axis, count, groups=None):
-    copies = jnp.broadcast_to(array[None], (count,) + array.shape)
-    return lax.all_to_all(copies, axis, 0, 0, axis_index_groups=groups)
 
 
 def make_on_device(n_seq, n_head):
@@ -221,22 +219,23 @@
 
     def on_device(tokens, norm_gain, w_qkv, w_out, span_order, frame_id, camera_id):
         columns = tokens.shape[1]
-        gathered = send_to_all(tokens, "head", n_head)
+        copies = jnp.broadcast_to(tokens[None], (n_head,) + tokens.shape)
+        gathered = lax.all_to_all(copies, "head", 0, 0)
         query_code, key_code = codes(span_order, frame_id, camera_id)
         w_split = w_out.reshape(HD, n_head, columns).transpose(1, 0, 2)
         gathered, w_split, query_code, key_code = lax.optimization_barrier(
             (gathered, w_split, query_code, key_code)
         )
         w_columns = lax.all_to_all(w_split, "head", 0, 0)
-        queries, kv = project(gathered, norm_gain.reshape(1, D), w_qkv.transpose(1, 0, 2))
+        queries, kv = project(gathered, norm_gain.reshape(1, D), w_qkv.transpose(1, 0, 2), blocks)
         all_queries = lax.all_gather(queries, "seq", axis_index_groups=near)
         all_queries, kv, w_columns = lax.optimization_barrier((all_queries, kv, w_columns))
-        own_kv = send_to_all(kv, "seq", blocks, far)
+        own_kv = lax.all_to_all(kv, "seq", 0, 0, axis_index_groups=far)
         other_kv = lax.ppermute(own_kv, "seq", swap)
         parts = attend(all_queries, query_code, own_kv, other_kv, key_code)
         parts = lax.all_to_all(parts, "seq", 0, 0, axis_index_groups=near)
-        attended = combine(parts)
-        all_attended = send_to_all(attended, "head", n_head)
+        attended = combine(parts, n_head)
+        all_attended = lax.all_to_all(attended, "head", 0, 0)
         return output(all_attended, w_columns)
 
     return on_device

time: 148 us -> 150 us (1.014)
    unnamed x15 -> x17, local copies, waits for them, and re-layouts: 3.55 us -> 4.37 us
where the time goes in v3:
time: 150 us; the launch traced here: 149 us
  blocking collectives  88.7 us (59%)
  waiting for transfers between devices  23.5 us (16%)
  starting transfers between devices  17.5 us (12%)
  local copies, waits for them, and re-layouts  10.1 us (7%)
  Pallas kernels  9.02 us (6%)
    all_to_all x1, blocking collectives, on_device(): own_kv = lax.all_to_all(kv, 'seq', 0, 0, axis_index_groups=far)  37.5 us
    all_to_all x1, blocking collectives, on_device(): all_attended = lax.all_to_all(attended, 'head', 0, 0)  21.7 us
    all_to_all x1, waiting for transfers between devices, on_device(): gathered = lax.all_to_all(copies, 'head', 0, 0)  21.7 us
    all_gather x1, blocking collectives, on_device(): all_queries = lax.all_gather(queries, 'seq', axis_index_groups=near)  15.8 us
    all_to_all x1, blocking collectives, on_device(): parts = lax.all_to_all(parts, 'seq', 0, 0, axis_index_groups=near)  13.7 us
    all_to_all x1, starting transfers between devices, on_device(): gathered = lax.all_to_all(copies, 'head', 0, 0)  9.4 us
    all_to_all x1, starting transfers between devices, on_device(): w_columns = lax.all_to_all(w_split, 'head', 0, 0)  6.22 us
    pallas_call x1, Pallas kernels, attend(): pl.pallas_call(attend_kernel, grid=(groups,), in_specs=[pl.BlockSpec((1,...  4.95 us
  transfers between devices with their start and end apart: 3, of which 2 were waited for; matrix products, arithmetic and copies ran while one was open for 2% of the time, Pallas kernels for 2%

profile of v3, /device:TPU:6, one launch (start us, length us, event | category | flops | bytes accessed | tf_op | source)
XLA Modules:
  0.0 149.2 jit_solution(7928354004792765179)
XLA Ops:
  0.0 2.4 %broadcast_in_dim.8 = bf16[16,256,256]{2,1,0:T(8,128)(2,1)} broadcast(bf16[256,256]{1,0:T(8,128)(2,1)} %param.7), dimensions={1,2} | broadcast | bytes 2228224 | tf_op jit(solution)/shard_map/broadcast_in_dim | solution.py:222
  2.4 9.4 %all-to-all-start = ((bf16[16,256,256]{2,1,0:T(8,128)(2,1)}), bf16[16,256,256]{2,1,0:T(8,128)(2,1)S(1)}, u32[]{:S(2)}, u32[]{:S(2)}) async-start(bf16[16,256,256]{2,1,0:T(8,128)(2,1)} %broadcast_in_dim.8), calls=%async_computation | async-start | bytes 4194304 | tf_op jit(solution)/shard_map/all_to_all | solution.py:223
  11.9 0.0 copy-start.4
  11.9 0.0 copy-start.5
  11.9 1.6 %copy.8 = bf16[128,4096]{0,1:T(8,128)(2,1)S(1)} copy(bf16[128,4096]{1,0:T(8,128)(2,1)} %param.10) | data formatting | bytes 2097152 | tf_op args[3]
  13.5 1.3 copy.9
  14.9 0.6 gather_fusion
  15.6 21.7 %all-to-all-done.x_ref = bf16[16,256,256]{2,1,0:T(8,128)(2,1)S(1)} async-done(((bf16[16,256,256]{2,1,0:T(8,128)(2,1)}), bf16[16,256,256]{2,1,0:T(8,128)(2,1)S(1)}, u32[]{:S(2)}, u32[]{:S(2)}) %all-to-all-start) | async-done | bytes 2097184 | tf_op jit(solution)/shard_map/all_to_all | solution.py:223
  37.3 1.3 broadcast_in_dim.20.kcode_ref
  38.6 6.2 %all-to-all-start.1 = ((bf16[16,128,256]{2,1,0:T(8,128)(2,1)}), bf16[16,128,256]{2,1,0:T(8,128)(2,1)S(1)}, u32[]{:S(2)}, u32[]{:S(2)}) async-start(bf16[16,128,256]{2,1,0:T(8,128)(2,1)} %bitcast.19), calls=%async_computation.1 | async-start | bytes 2097152 | tf_op jit(solution)/shard_map/all_to_all | solution.py:229
  44.8 0.0 copy-start.1
  44.9 1.9 %copy-done.1 = bf16[4096,3,128]{2,0,1:T(8,128)(2,1)S(1)} copy-done((bf16[4096,3,128]{2,0,1:T(8,128)(2,1)S(1)}, bf16[4096,3,128]{2,0,1:T(8,128)(2,1)}, u32[]{:S(2)}) %copy-start.1) | copy-done | bytes 3145752
  46.7 2.5 %project.1 = (bf16[256,128]{1,0:T(8,128)(2,1)S(1)}, bf16[4,256,256]{2,1,0:T(8,128)(2,1)S(1)}) custom-call(bf16[16,256,256]{2,1,0:T(8,128)(2,1)S(1)} %all-to-all-done.x_ref, f32[1,4096]{1,0:T(1,128)S(1)} %bitcast.18, bf16[3,4096,128]{2,1,0:T(8,128)(2,1)S(1)} %bitcast.16), custom_call_target="tpu_custom_call" | custom-call | tf_op jit(solution)/shard_map/project/pallas_call | solution.py:62
  49.2 0.8 copy-done.2
  50.1 15.8 %all-gather = bf16[1024,128]{1,0:T(8,128)(2,1)S(1)} all-gather(bf16[256,128]{1,0:T(8,128)(2,1)S(1)} %get-tuple-element.15), channel_id=2, replica_groups={{0,32,64,96},{16,48,80,112},{128,160,192,224},{144,176,208,240},{256,28..., dimensions={0}, use_global_device_ids=true | all-gather | bytes 327680 | tf_op jit(solution)/shard_map/all_gather | solution.py:231
  65.9 0.0 all-to-all-done.1.w_ref
  65.9 37.5 %all_to_all.25.own_ref = bf16[4,256,256]{2,1,0:T(8,128)(2,1)S(1)} all-to-all(bf16[4,256,256]{2,1,0:T(8,128)(2,1)} %copy-done.2), channel_id=1, replica_groups={{0,128,256,384},{16,144,272,400},{32,160,288,416},{48,176,304,432},{64,..., dimensions={0} | all-to-all | bytes 1048576 | tf_op jit(solution)/shard_map/all_to_all | solution.py:233
  103.4 1.9 %collective-permute-start = (bf16[4,256,256]{2,1,0:T(8,128)(2,1)S(1)}, bf16[4,256,256]{2,1,0:T(8,128)(2,1)S(1)}, u32[]{:S(2)}, u32[]{:S(2)}) collective-permute-start(bf16[4,256,256]{2,1,0:T(8,128)(2,1)S(1)} %all_to_all.25.own_ref), channel_id=1, source_target_pairs={{0,16},{16,0},{32,48},{48,32},{64,80},{80,64},{96,112},{112,96},{1... | collective-permute-start | bytes 1572872 | tf_op jit(solution)/shard_map/ppermute | solution.py:234
  105.3 1.9 %collective-permute-done.other_ref = bf16[4,256,256]{2,1,0:T(8,128)(2,1)S(1)} collective-permute-done((bf16[4,256,256]{2,1,0:T(8,128)(2,1)S(1)}, bf16[4,256,256]{2,1,0:T(8,128)(2,1)S(1)}, u32[]{:S(2)}, u32[]{:S(2)}) %collective-permute-start) | collective-permute-done | bytes 524320 | tf_op jit(solution)/shard_map/ppermute | solution.py:234
  107.2 5.0 %attend.1 = bf16[4,144,256]{2,1,0:T(8,128)(2,1)S(1)} custom-call(bf16[4,256,128]{2,1,0:T(8,128)(2,1)S(1)} %bitcast.17, s32[4,1,256]{2,1,0:T(1,128)S(1)} %dynamic-slice_bitcast_fusion.qcode_ref, bf16[4,256,256]{2,1,0:T(8,128)(2,1)S(1)} %all_to_all.25.own_ref, bf16[4,256,256]{2,1,0:T(8,128)(2,1)S(1)} %collective-permute-done.other_ref, s32[2048,128]{1,0:T(8,128)S(1)} %copy-done), custom_call_target="tpu_custom_call" | custom-call | tf_op jit(solution)/shard_map/attend/pallas_call | solution.py:133
  112.1 13.7 %all_to_all.26.part_ref = bf16[4,144,256]{2,1,0:T(8,128)(2,1)S(1)} all-to-all(bf16[4,144,256]{2,1,0:T(8,128)(2,1)S(1)} %attend.1), channel_id=1, replica_groups={{0,32,64,96},{16,48,80,112},{128,160,192,224},{144,176,208,240},{256,28..., dimensions={0} | all-to-all | bytes 589824 | tf_op jit(solution)/shard_map/all_to_all | solution.py:236
  125.8 0.2 combine.1
  126.1 21.7 %all_to_all.27.attended_ref = bf16[16,256,128]{2,1,0:T(8,128)(2,1)S(1)} all-to-all(bf16[16,256,128]{2,1,0:T(8,128)(2,1)S(1)} %combine.1), channel_id=1, replica_groups=mesh['seq'=32,'head'=16] {'head'}, dimensions={0} | all-to-all | bytes 2097152 | tf_op jit(solution)/shard_map/all_to_all | solution.py:238
  147.8 1.4 output.1
  (18 shorter events, 0.1 us)
Async XLA Ops:
  2.4 34.9 %all-to-all-start = ((bf16[16,256,256]{2,1,0:T(8,128)(2,1)}), bf16[16,256,256]{2,1,0:T(8,128)(2,1)S(1)}, u32[]{:S(2)}, u32[]{:S(2)}) async-start(bf16[16,256,256]{2,1,0:T(8,128)(2,1)} %broadcast_in_dim.8), calls=%async_computation | async-start | bytes 4194304 | tf_op jit(solution)/shard_map/all_to_all | solution.py:223
  11.8 3.0 %copy-start.6 = (s32[64]{0:T(128)S(1)}, s32[64]{0:T(128)}, u32[]{:S(2)}) copy-start(s32[64]{0:T(128)} %param.11) | copy-start | bytes 772
  11.9 3.0 %copy-start.4 = (s32[8192]{0:T(1024)S(1)}, s32[8192]{0:T(1024)}, u32[]{:S(2)}) copy-start(s32[8192]{0:T(1024)} %param.13) | copy-start | bytes 98308
  11.9 3.0 %copy-start.5 = (s32[8192]{0:T(1024)S(1)}, s32[8192]{0:T(1024)}, u32[]{:S(2)}) copy-start(s32[8192]{0:T(1024)} %param.12) | copy-start | bytes 98308
  14.8 30.0 %copy-start.3 = (f32[4096]{0:T(1024)S(1)}, f32[4096]{0:T(1024)}, u32[]{:S(2)}) copy-start(f32[4096]{0:T(1024)} %param.8) | copy-start | bytes 49156
  38.6 27.2 %all-to-all-start.1 = ((bf16[16,128,256]{2,1,0:T(8,128)(2,1)}), bf16[16,128,256]{2,1,0:T(8,128)(2,1)S(1)}, u32[]{:S(2)}, u32[]{:S(2)}) async-start(bf16[16,128,256]{2,1,0:T(8,128)(2,1)} %bitcast.19), calls=%async_computation.1 | async-start | bytes 2097152 | tf_op jit(solution)/shard_map/all_to_all | solution.py:229
  44.8 1.9 %copy-start.1 = (bf16[4096,3,128]{2,0,1:T(8,128)(2,1)S(1)}, bf16[4096,3,128]{2,0,1:T(8,128)(2,1)}, u32[]{:S(2)}) copy-start(bf16[4096,3,128]{2,0,1:T(8,128)(2,1)} %param.9) | copy-start | bytes 9437188
  49.2 0.8 copy-start.2
  50.1 57.1 %copy-start = (s32[2048,128]{1,0:T(8,128)S(1)}, s32[2048,128]{1,0:T(8,128)}, u32[]{:S(2)}) copy-start(s32[2048,128]{1,0:T(8,128)} %broadcast_in_dim.20.kcode_ref) | copy-start | bytes 3145732
  103.4 3.8 %collective-permute-start = (bf16[4,256,256]{2,1,0:T(8,128)(2,1)S(1)}, bf16[4,256,256]{2,1,0:T(8,128)(2,1)S(1)}, u32[]{:S(2)}, u32[]{:S(2)}) collective-permute-start(bf16[4,256,256]{2,1,0:T(8,128)(2,1)S(1)} %all_to_all.25.own_ref), channel_id=1, source_target_pairs={{0,16},{16,0},{32,48},{48,32},{64,80},{80,64},{96,112},{112,96},{1... | collective-permute-start | bytes 1572872 | tf_op jit(solution)/shard_map/ppermute | solution.py:234
